TPU v7x, 256 devices: a whole 4x4x8 slice. The times are simulated.
256 devices in a mesh: ctxa: 32 (over x, z), ctxb: 8 (over y, core).
Axes of the slice: x: 4, y: 4, z: 8, core: 2. Of those that a mesh axis runs over, the one named last changes fastest.
Arguments:
- tokens: bfloat16 [32768, 1024], P(('ctxa', 'ctxb')), may hold values from -80 to 80
- w_query: bfloat16 [1024, 512], replicated, may hold values from -0.1875 to 0.1875
- w_key: bfloat16 [1024, 512], replicated, may hold values from -0.1875 to 0.1875
- w_value: bfloat16 [1024, 512], replicated, may hold values from -0.1875 to 0.1875
- w_slot: bfloat16 [8, 64, 128], replicated, may hold values from -3 to 3
- w_out: bfloat16 [512, 1024], replicated, may hold values from -1 to 1
Outputs:
- mixed: bfloat16 [32768, 1024], P(('ctxa', 'ctxb'))
All inputs are finite; a program needn't handle non-finite values.
Results may differ from a plain program's by a relative error of at most 0.012.
The roundings to bfloat16 on the way count: a program that leaves them out, or rounds other values in their place, can miss the bound.
Values may be sent and summed in bfloat16 or wider, within the bound.
A program may use at most 192 MiB of HBM per device.

v0:
```python
import jax
import jax.numpy as jnp
from jax import lax
from jax.sharding import PartitionSpec as P

HEADS = 8
HEAD_DIM = 64
SLOTS = 128
WINDOW = 128


def padded_2(block, sides, width):
    for axis, dim in sides:
        count = lax.axis_size(axis)
        forward = [(i, i + 1) for i in range(count - 1)]
        backward = [(target, source) for source, target in forward]
        low = lax.ppermute(
            lax.slice_in_dim(block, block.shape[dim] - width, None, axis=dim), axis, forward
        )
        high = lax.ppermute(lax.slice_in_dim(block, 0, width, axis=dim), axis, backward)
        block = jnp.concatenate([low, block, high], axis=dim)
    return block


def layer_norm(values):
    center = values - jnp.mean(values, axis=-1, keepdims=True)
    spread = jnp.mean(center * center, axis=-1, keepdims=True)
    return center * lax.rsqrt(spread + 1e-05)


def finish_slots(total, sums):
    slot_keys = layer_norm(sums[..., :HEAD_DIM]).astype(jnp.bfloat16)
    slot_values = (sums[..., HEAD_DIM:] / total[..., None]).astype(jnp.bfloat16)
    return (slot_keys, slot_values)


def per_device(tokens, w_query, w_key, w_value, w_slot, w_out):
    rows = tokens.shape[0]
    width = HEADS * HEAD_DIM
    query = jnp.dot(tokens, w_query, preferred_element_type=jnp.float32).astype(jnp.bfloat16)
    key = jnp.dot(tokens, w_key, preferred_element_type=jnp.float32).astype(jnp.bfloat16)
    value = jnp.dot(tokens, w_value, preferred_element_type=jnp.float32).astype(jnp.bfloat16)
    key_heads = key.reshape(rows, HEADS, HEAD_DIM)
    logits = jnp.einsum("thd,hds->hts", key_heads, w_slot, preferred_element_type=jnp.float32)
    paired = jnp.concatenate([key_heads, value.reshape(rows, HEADS, HEAD_DIM)], axis=2).astype(
        jnp.float32
    )
    local_top = jnp.max(logits, axis=1)
    top = lax.pmax(local_top, ("ctxa", "ctxb"))
    weight = jnp.exp(logits - top[:, None, :])
    total = jnp.sum(weight, axis=1)
    sums = jnp.einsum("hts,thd->hsd", weight, paired, precision=lax.Precision.HIGHEST)
    total, sums = lax.psum((total, sums), ("ctxa", "ctxb"))
    slot_keys, slot_values = finish_slots(total, sums)
    near_keys = layer_norm(key_heads.astype(jnp.float32)).astype(jnp.bfloat16).reshape(rows, width)
    stacked = jnp.concatenate([near_keys, value], axis=1)
    padded = padded_2(stacked, ((("ctxa", "ctxb"), 0),), WINDOW)
    seq_len = rows * lax.axis_size(("ctxa", "ctxb"))
    offset = lax.axis_index(("ctxa", "ctxb")) * rows
    block = min(512, rows)
    span = block + 2 * WINDOW
    scale = 1.0 / HEAD_DIM**0.5
    groups = 2
    group_heads = HEADS // groups
    group_width = group_heads * HEAD_DIM
    grouped_keys = slot_keys.reshape(groups, group_heads, SLOTS, HEAD_DIM)
    grouped_values = slot_values.reshape(groups, group_heads, SLOTS, HEAD_DIM)
    blocks = rows // block

    def attend(item):
        index = item // groups
        group = item % groups
        start = index * block
        column = group * group_width
        query_block = lax.dynamic_slice_in_dim(query, column, group_width, 1).reshape(
            block, group_heads, HEAD_DIM
        )
        keys_block = lax.dynamic_slice_in_dim(padded, column, group_width, 1).reshape(
            span, group_heads, HEAD_DIM
        )
        values_block = lax.dynamic_slice_in_dim(padded, width + column, group_width, 1).reshape(
            span, group_heads, HEAD_DIM
        )
        group_slot_keys = lax.dynamic_index_in_dim(grouped_keys, group, 0, keepdims=False)
        group_slot_values = lax.dynamic_index_in_dim(grouped_values, group, 0, keepdims=False)
        query_pos = offset + start + jnp.arange(block, dtype=jnp.int32)
        key_pos = offset + start - WINDOW + jnp.arange(span, dtype=jnp.int32)
        valid = (
            (jnp.abs(key_pos[None, :] - query_pos[:, None]) <= WINDOW)
            & (key_pos[None, :] >= 0)
            & (key_pos[None, :] < seq_len)
        )
        near = (
            jnp.einsum("bhd,khd->hbk", query_block, keys_block, preferred_element_type=jnp.float32)
            * scale
        )
        near = jnp.where(valid[None], near, -1e30)
        far = (
            jnp.einsum(
                "bhd,hsd->hbs", query_block, group_slot_keys, preferred_element_type=jnp.float32
            )
            * scale
        )
        top_score = jnp.maximum(jnp.max(near, axis=-1), jnp.max(far, axis=-1))
        near_exp = jnp.exp(near - top_score[..., None])
        far_exp = jnp.exp(far - top_score[..., None])
        denom = jnp.sum(near_exp, axis=-1) + jnp.sum(far_exp, axis=-1)
        near_probs = (near_exp / denom[..., None]).astype(jnp.bfloat16)
        far_probs = (far_exp / denom[..., None]).astype(jnp.bfloat16)
        result = jnp.einsum(
            "hbk,khd->bhd", near_probs, values_block, preferred_element_type=jnp.float32
        )
        result = result + jnp.einsum(
            "hbs,hsd->bhd", far_probs, group_slot_values, preferred_element_type=jnp.float32
        )
        return result.reshape(block, group_width).astype(jnp.bfloat16)

    pieces = lax.map(attend, jnp.arange(blocks * groups, dtype=jnp.int32))
    attended = (
        pieces.reshape(blocks, groups, block, group_width)
        .transpose(0, 2, 1, 3)
        .reshape(rows, width)
    )
    return jnp.dot(attended, w_out, preferred_element_type=jnp.float32).astype(jnp.bfloat16)


def solution(mesh):
    in_specs = (P(("ctxa", "ctxb"), None), P(), P(), P(), P(), P())
    out_specs = P(("ctxa", "ctxb"), None)
    return jax.shard_map(
        per_device, mesh=mesh, in_specs=in_specs, out_specs=out_specs, check_vma=False
    )
```

profile of v0, /device:TPU:2, one launch (start us, length us, event | category | flops | bytes accessed | tf_op | source)
XLA Modules:
  0.0 378.1 jit_solution(4458475252980913308)
XLA Ops:
  6.5 0.0 copy-start
  6.5 0.0 copy-start.2
  6.5 0.0 copy-start.3
  6.5 0.0 all-reduce.2.cloned.1.call-start
  6.5 1.8 convolution_convert_fusion.3
  8.3 0.1 copy.17
  8.4 0.0 copy-done.2
  8.4 0.0 copy-done.3
  8.5 0.3 convolution_convert_fusion.2
  8.9 0.1 copy.19
  9.1 0.1 copy.18
  9.2 0.0 copy-start.5
  9.2 0.1 multiply_convert_fusion.1
  9.3 0.7 pad_maximum_fusion.1
  10.0 1.9 collective-permute-start
  11.9 9.6 %collective-permute-start.1 = (bf16[128,1024]{1,0:T(8,128)(2,1)}, bf16[128,1024]{1,0:T(8,128)(2,1)}, u32[]{:S(2)}, u32[]{:S(2)}) collective-permute-start(bf16[128,1024]{1,0:T(8,128)(2,1)} %pad_maximum_fusion.1), channel_id=1, source_target_pairs={{1,0},{2,1},{3,2},{4,3},{5,4},{6,5},{7,6},{8,7},{9,8},{10,9},{11,1... | collective-permute-start | bytes 786440 | tf_op jit(solution)/shard_map/ppermute | solution.py:20
  21.6 0.1 copy.20
  21.7 0.9 copy.21
  22.6 0.0 copy-done.5
  22.6 0.3 fusion.27
  22.8 72.5 %pmax.7 = f32[8,128]{1,0:T(8,128)S(1)} all-reduce(f32[8,128]{1,0:T(8,128)S(1)} %get-tuple-element.154), channel_id=1, replica_groups=mesh['ctxa'=32,'ctxb'=8] {'ctxa','ctxb'}, use_global_device_ids=true, to_apply=%region_3.0 | all-reduce | flops 1024 | bytes 8192 | tf_op jit(solution)/shard_map/pmax | solution.py:49
  95.3 0.2 copy.22
  95.5 0.0 copy-start.4
  95.5 2.5 fusion.17
  98.0 0.0 all-reduce.2.cloned.1.call-update
  98.0 0.1 fusion.16
  98.1 75.0 %psum.15 = f32[8,128]{1,0:T(8,128)S(1)} all-reduce(f32[8,128]{1,0:T(8,128)S(1)} %fusion.16), channel_id=1, replica_groups=mesh['ctxa'=32,'ctxb'=8] {'ctxa','ctxb'}, use_global_device_ids=true, to_apply=%region_8.0 | all-reduce | flops 1024 | bytes 8192 | tf_op jit(solution)/shard_map/psum | solution.py:53
  173.1 0.0 copy-done.4
  173.1 0.3 convolution_convert_fusion.1
  173.5 179.0 %all-reduce.2.cloned.1.call-done = f32[8,128,128]{2,1,0:T(8,128)} async-done(((f32[8,128,128]{2,1,0:T(8,128)}), f32[8,128,128]{2,1,0:T(8,128)}) %all-reduce.2.cloned.1.call-update) | async-done | bytes 524304 | tf_op jit(solution)/shard_map/psum | solution.py:53
  352.4 0.0 copy-start.1
  352.4 1.3 slice_reduce_fusion
  353.8 1.4 multiply_reduce_fusion
  355.2 0.0 copy-done.1
  355.2 0.6 fusion.15
  355.8 0.1 copy.26
  356.0 0.1 copy.27
  356.1 0.0 collective-permute-done
  356.1 0.0 collective-permute-done.1
  356.1 1.1 pad_maximum_fusion
  357.2 0.4 copy.24
  357.6 11.7 %while.12 = (s32[]{:T(128)}, bf16[2,128,256]{1,2,0:T(8,128)(2,1)}, s32[2]{0:T(128)S(1)}, bf16[384,1024]{0,1:T(8,128)(2,1)S(1)}, s32[]{:T(128)}, /*index=5*/bf16[...) while((s32[]{:T(128)}, bf16[2,128,256]{1,2,0:T(8,128)(2,1)}, ...), condition=%wide.region_14.15_spmd, body=%wide.region_9.14_spmd.sunk | while | flops 69452448 | bytes 5446203 | solution.py:118
  357.6 0.6 dynamic_slice.60
  360.9 0.1 fusion.62
  361.1 0.1 copy.32
  361.2 0.4 fusion.63
  361.6 0.3 fusion.60
  361.9 0.1 fusion.65
  362.0 0.3 fusion.64
  362.3 0.2 fusion.66
  362.4 0.4 fusion.67
  362.8 0.6 constant_dynamic-update-slice_fusion.2
  363.5 0.6 dynamic_slice.60
  366.8 0.1 fusion.62
  366.9 0.1 copy.32
  367.1 0.4 fusion.63
  367.5 0.3 fusion.60
  367.7 0.1 fusion.65
  367.8 0.3 fusion.64
  368.1 0.2 fusion.66
  368.3 0.4 fusion.67
  368.7 0.6 constant_dynamic-update-slice_fusion.2
  369.3 0.0 copy-done
  369.3 1.9 convolution_convert_fusion
  (24 shorter events, 0.3 us)
Async XLA Ops:
  6.5 362.8 %copy-start = (bf16[512,1024]{1,0:T(8,128)(2,1)S(1)}, bf16[512,1024]{1,0:T(8,128)(2,1)}, u32[]{:S(2)}) copy-start(bf16[512,1024]{1,0:T(8,128)(2,1)} %param.13) | copy-start | bytes 3145732
  6.5 1.9 copy-start.2
  6.5 1.9 copy-start.3
  6.5 345.9 %all-reduce.2.cloned.1.call-start = ((), (), s32[]{:S(2)}) async-start(), calls=%async_computation | async-start | bytes 1048576 | tf_op jit(solution)/shard_map/psum | solution.py:53
  9.2 13.3 %copy-start.5 = (bf16[8,64,128]{2,1,0:T(8,128)(2,1)S(1)}, bf16[8,64,128]{2,1,0:T(8,128)(2,1)}, u32[]{:S(2)}) copy-start(bf16[8,64,128]{2,1,0:T(8,128)(2,1)} %param.12) | copy-start | bytes 393220
  10.0 346.1 %collective-permute-start = (bf16[128,1024]{1,0:T(8,128)(2,1)}, bf16[128,1024]{1,0:T(8,128)(2,1)}, u32[]{:S(2)}, u32[]{:S(2)}) collective-permute-start(bf16[128,1024]{1,0:T(8,128)(2,1)} %pad_maximum_fusion.1), channel_id=1, source_target_pairs={{0,1},{1,2},{2,3},{3,4},{4,5},{5,6},{6,7},{7,8},{8,9},{9,10},{10,1... | collective-permute-start | bytes 786440 | tf_op jit(solution)/shard_map/ppermute | solution.py:17
  11.9 344.2 %collective-permute-start.1 = (bf16[128,1024]{1,0:T(8,128)(2,1)}, bf16[128,1024]{1,0:T(8,128)(2,1)}, u32[]{:S(2)}, u32[]{:S(2)}) collective-permute-start(bf16[128,1024]{1,0:T(8,128)(2,1)} %pad_maximum_fusion.1), channel_id=1, source_target_pairs={{1,0},{2,1},{3,2},{4,3},{5,4},{6,5},{7,6},{8,7},{9,8},{10,9},{11,1... | collective-permute-start | bytes 786440 | tf_op jit(solution)/shard_map/ppermute | solution.py:20
  95.5 77.7 %copy-start.4 = (bf16[1024,512]{1,0:T(8,128)(2,1)S(1)}, bf16[1024,512]{1,0:T(8,128)(2,1)}, u32[]{:S(2)}) copy-start(bf16[1024,512]{1,0:T(8,128)(2,1)} %param.9) | copy-start | bytes 3145732
  352.4 2.8 copy-start.1
Sparse Core Ops, SparseCore 0:
  98.2 254.2 all-reduce.1
where the time goes:
time: 379 us; the launch traced here: 378 us
  waiting for transfers between devices  179 us (47%)
  blocking collectives  147 us (39%)
  between operations  13.7 us (4%)
  starting transfers between devices  11.5 us (3%)
  matrix products  9.54 us (3%)
  other arithmetic  6.44 us (2%)
  loops' own time  5.47 us (1%)
  local copies, waits for them, and re-layouts  4.99 us (1%)
    psum x1, waiting for transfers between devices, per_device(): total, sums = lax.psum((total, sums), ('ctxa', 'ctxb'))  179 us
    psum x1, blocking collectives, per_device(): total, sums = lax.psum((total, sums), ('ctxa', 'ctxb'))  75 us
    pmax x1, blocking collectives, per_device(): top = lax.pmax(local_top, ('ctxa', 'ctxb'))  72.5 us
    ppermute x1, starting transfers between devices, padded_2(): lax.ppermute(lax.slice_in_dim(block, 0, width, axis=dim), axis, backward)  9.63 us
  transfers between devices with their start and end apart: 3, of which 1 were waited for; matrix products, arithmetic and copies ran while one was open for 2% of the time, Pallas kernels for 0%

commit v1 on v0

--- a/solution.py
+++ b/solution.py
@@ -50,7 +50,7 @@
     weight = jnp.exp(logits - top[:, None, :])
     total = jnp.sum(weight, axis=1)
     sums = jnp.einsum("hts,thd->hsd", weight, paired, precision=lax.Precision.HIGHEST)
-    total, sums = lax.psum((total, sums), ("ctxa", "ctxb"))
+    total, sums = lax.psum(lax.psum((total, sums), axis_name="ctxa"), axis_name="ctxb")
     slot_keys, slot_values = finish_slots(total, sums)
     near_keys = layer_norm(key_heads.astype(jnp.float32)).astype(jnp.bfloat16).reshape(rows, width)
     stacked = jnp.concatenate([near_keys, value], axis=1)

time: 379 us -> 347 us (0.916)
  the two profiles are of different devices: /device:TPU:2 before, /device:TPU:1 now
where the time goes in v1:
time: 347 us
  blocking collectives  171 us (49%)
  waiting for transfers between devices  134 us (39%)
  between operations  13.7 us (4%)
  matrix products  8.49 us (2%)
  loops' own time  5.81 us (2%)
  other arithmetic  4.7 us (1%)
  starting transfers between devices  4.51 us (1%)
  local copies, waits for them, and re-layouts  4.48 us (1%)
    psum x1, waiting for transfers between devices, per_device(): lax.psum((total, sums), axis_name='ctxa')  134 us
    pmax x1, blocking collectives, per_device(): top = lax.pmax(local_top, ('ctxa', 'ctxb'))  81.4 us
    psum x1, blocking collectives, per_device(): lax.psum((total, sums), axis_name='ctxa')  58.4 us
    psum x1, blocking collectives, per_device(): lax.psum(lax.psum((total, sums), axis_name='ctxa'), axis_name='ctxb')  30.9 us
  transfers between devices with their start and end apart: 4, of which 1 were waited for; matrix products, arithmetic and copies ran while one was open for 0% of the time, Pallas kernels for 0%

profile of v1, /device:TPU:1, one launch (start us, length us, event | category | flops | bytes accessed | tf_op | source)
XLA Modules:
  0.0 346.7 jit_solution(1086859893066846800)
XLA Ops:
  6.5 0.0 copy-start
  6.5 0.0 all-reduce.3.cloned.1.call-start
  6.5 1.7 convolution_convert_fusion.3
  8.3 0.0 copy-start.2
  8.3 0.0 copy-start.3
  8.3 0.1 copy.17
  8.4 0.2 copy.21
  8.6 0.0 copy-done.5
  8.6 0.3 fusion.27
  8.9 81.4 %pmax.7 = f32[8,128]{1,0:T(8,128)S(1)} all-reduce(f32[8,128]{1,0:T(8,128)S(1)} %get-tuple-element.154), channel_id=1, replica_groups=mesh['ctxa'=32,'ctxb'=8] {'ctxa','ctxb'}, use_global_device_ids=true, to_apply=%region_3.0 | all-reduce | flops 1024 | bytes 8192 | tf_op jit(solution)/shard_map/pmax | solution.py:49
  90.3 0.0 copy-done.2
  90.3 0.0 copy-done.3
  90.3 0.3 convolution_convert_fusion.2
  90.6 0.1 copy.20
  90.7 0.2 copy.22
  90.9 1.5 fusion.17
  92.4 0.0 all-reduce.3.cloned.1.call-update
  92.5 0.0 all-reduce.5.cloned.1.call-start
  92.6 0.1 copy.19
  92.8 0.1 copy.18
  92.9 0.0 copy-start.4
  93.0 0.1 multiply_convert_fusion.1
  93.0 2.1 collective-permute-start
  95.1 2.4 collective-permute-start.1
  97.5 0.0 copy-done.4
  97.5 0.3 convolution_convert_fusion.1
  97.9 134.1 %all-reduce.3.cloned.1.call-done = f32[8,128,128]{2,1,0:T(8,128)} async-done(((f32[8,128,128]{2,1,0:T(8,128)}), f32[8,128,128]{2,1,0:T(8,128)}) %all-reduce.3.cloned.1.call-update) | async-done | bytes 524304 | tf_op jit(solution)/shard_map/psum | solution.py:53
  232.0 0.0 all-reduce.5.cloned.1.call-update
  232.0 0.1 fusion.16
  232.1 58.4 %psum.30 = f32[8,128]{1,0:T(8,128)S(1)} all-reduce(f32[8,128]{1,0:T(8,128)S(1)} %fusion.16), channel_id=1, replica_groups=mesh['ctxa'=32,'ctxb'=8] {'ctxa'}, use_global_device_ids=true, to_apply=%region_9.0 | all-reduce | flops 1024 | bytes 8192 | tf_op jit(solution)/shard_map/psum | solution.py:53
  290.6 30.9 %psum.31 = f32[8,128]{1,0:T(8,128)S(1)} all-reduce(f32[8,128]{1,0:T(8,128)S(1)} %psum.30), channel_id=1, replica_groups=mesh['ctxa'=32,'ctxb'=8] {'ctxb'}, use_global_device_ids=true, to_apply=%region_10.0 | all-reduce | flops 1024 | bytes 8192 | tf_op jit(solution)/shard_map/psum | solution.py:53
  321.5 0.0 collective-permute-done
  321.5 0.0 collective-permute-done.1
  321.5 0.1 pad_maximum_fusion
  321.6 0.4 copy.24
  322.0 0.0 all-reduce.5.cloned.1.call-done
  322.0 1.3 slice_reduce_fusion
  323.3 1.4 multiply_reduce_fusion
  324.8 0.6 fusion.15
  325.4 0.1 copy.26
  325.5 0.1 copy.27
  325.7 12.2 %while.12 = (s32[]{:T(128)}, bf16[2,128,256]{1,2,0:T(8,128)(2,1)}, s32[2]{0:T(128)S(1)}, bf16[384,1024]{0,1:T(8,128)(2,1)S(1)}, s32[]{:T(128)}, /*index=5*/bf16[...) while((s32[]{:T(128)}, bf16[2,128,256]{1,2,0:T(8,128)(2,1)}, ...), condition=%wide.region_16.17_spmd, body=%wide.region_11.16_spmd.sunk | while | flops 69452448 | bytes 5446203 | solution.py:118
  325.7 0.7 dynamic_slice.60
  329.3 0.1 fusion.62
  329.4 0.1 copy.32
  329.5 0.4 fusion.63
  329.9 0.3 fusion.60
  330.2 0.1 fusion.65
  330.3 0.3 fusion.64
  330.6 0.2 fusion.66
  330.8 0.4 fusion.67
  331.2 0.6 constant_dynamic-update-slice_fusion.2
  331.8 0.7 dynamic_slice.60
  335.3 0.1 fusion.62
  335.5 0.1 copy.32
  335.6 0.4 fusion.63
  336.0 0.3 fusion.60
  336.3 0.1 fusion.65
  336.4 0.3 fusion.64
  336.7 0.2 fusion.66
  336.9 0.4 fusion.67
  337.2 0.6 constant_dynamic-update-slice_fusion.2
  337.9 0.0 copy-done
  337.9 1.9 convolution_convert_fusion
  (28 shorter events, 0.3 us)
Async XLA Ops:
  6.5 331.3 %copy-start = (bf16[512,1024]{1,0:T(8,128)(2,1)S(1)}, bf16[512,1024]{1,0:T(8,128)(2,1)}, u32[]{:S(2)}) copy-start(bf16[512,1024]{1,0:T(8,128)(2,1)} %param.13) | copy-start | bytes 3145732
  6.5 2.1 copy-start.5
  6.5 225.5 %all-reduce.3.cloned.1.call-start = ((), (), s32[]{:S(2)}) async-start(), calls=%async_computation | async-start | bytes 1048576 | tf_op jit(solution)/shard_map/psum | solution.py:53
  8.3 82.0 %copy-start.2 = (bf16[128,1024]{1,0:T(8,128)(2,1)S(1)}, bf16[128,1024]{1,0:T(8,128)(2,1)}, u32[]{:S(2)}) copy-start(bf16[128,1024]{1,0:T(8,128)(2,1)} %param.8) | copy-start | bytes 786436
  8.3 82.0 %copy-start.3 = (bf16[1024,512]{1,0:T(8,128)(2,1)S(1)}, bf16[1024,512]{1,0:T(8,128)(2,1)}, u32[]{:S(2)}) copy-start(bf16[1024,512]{1,0:T(8,128)(2,1)} %param.11) | copy-start | bytes 3145732
  92.5 229.5 %all-reduce.5.cloned.1.call-start = ((), (), s32[]{:S(2)}) async-start(), calls=%async_computation.1 | async-start | bytes 1048576 | tf_op jit(solution)/shard_map/psum | solution.py:53
  92.9 4.6 %copy-start.4 = (bf16[1024,512]{1,0:T(8,128)(2,1)S(1)}, bf16[1024,512]{1,0:T(8,128)(2,1)}, u32[]{:S(2)}) copy-start(bf16[1024,512]{1,0:T(8,128)(2,1)} %param.9) | copy-start | bytes 3145732
  93.0 228.5 %collective-permute-start = (bf16[128,1024]{1,0:T(8,128)(2,1)S(1)}, bf16[128,1024]{1,0:T(8,128)(2,1)S(1)}, u32[]{:S(2)}, u32[]{:S(2)}) collective-permute-start(bf16[128,1024]{1,0:T(8,128)(2,1)S(1)} %pad_maximum_fusion.1), channel_id=1, source_target_pairs={{0,1},{1,2},{2,3},{3,4},{4,5},{5,6},{6,7},{7,8},{8,9},{9,10},{10,1... | collective-permute-start | bytes 786440 | tf_op jit(solution)/shard_map/ppermute | solution.py:17
  95.1 226.4 %collective-permute-start.1 = (bf16[128,1024]{1,0:T(8,128)(2,1)S(1)}, bf16[128,1024]{1,0:T(8,128)(2,1)S(1)}, u32[]{:S(2)}, u32[]{:S(2)}) collective-permute-start(bf16[128,1024]{1,0:T(8,128)(2,1)S(1)} %pad_maximum_fusion.1), channel_id=1, source_target_pairs={{1,0},{2,1},{3,2},{4,3},{5,4},{6,5},{7,6},{8,7},{9,8},{10,9},{11,1... | collective-permute-start | bytes 786440 | tf_op jit(solution)/shard_map/ppermute | solution.py:20
  322.0 2.8 copy-start.1
Sparse Core Ops, SparseCore 0:
  92.6 139.3 all-reduce.2
  234.4 65.6 all-reduce.4
